TPU v7x, 256 devices: a whole 4x4x8 slice. The times are simulated.
256 devices in a mesh: upd: 8 (over x, core), col: 32 (over z, y).
Axes of the slice: x: 4, y: 4, z: 8, core: 2. Of those that a mesh axis runs over, the one named last changes fastest.
Arguments:
- panel: bfloat16 [32, 8, 1024, 1024], P('col', None, 'upd'), may hold values from -6 to 6
- diag_tiles: bfloat16 [32, 1024, 1024], P('col', 'upd'), may hold values from -6 to 6
- dinv: bfloat16 [32, 1024, 1024], P('col'), may hold values from -1 to 1, as said below
- u_fac: bfloat16 [32, 8, 8, 96, 1024], P('col', None, 'upd'), may hold values from -1.1953125 to 1.1953125
- v_fac: bfloat16 [32, 8, 8, 96, 1024], P('col', None, 'upd'), may hold values from -1.1953125 to 1.1953125
- ranks: int32 [32, 8, 8], P('col', None, 'upd'), may hold values from 1 to 96, as said below
- sketch: bfloat16 [32, 64, 1024], P('col'), may hold values from -6 to 6
Outputs:
- panel_out: bfloat16 [32, 8, 1024, 1024], P('col', None, 'upd')
- diag_out: float32 [32, 1024, 1024], P('col', 'upd')
Inputs may be any that keep to these rules, and one draw needn't show every extreme that they name: `ranks`: in every panel tile at least two of the 8 pieces have rank 96. `dinv`: each block is lower triangular with a positive diagonal.
All inputs are finite; a program needn't handle non-finite values.
Results may differ from a plain program's by a relative error of at most 0.014.
Values may be sent and summed in bfloat16 or wider, within the bound.
No kernel may reach another device: no remote copies, remote signals or barrier semaphores. Data moves between devices by JAX's collectives and lax.ppermute only.
A program may use at most 64 MiB of HBM per device.

v0:
```python
import jax
import jax.numpy as jnp
from jax import lax
from jax.sharding import PartitionSpec as P


def in_blocks(array, dim, peers):
    dims = array.shape
    parts = array.reshape(*dims[:dim], peers, dims[dim] // peers, *dims[dim + 1 :])
    return jnp.moveaxis(parts, dim, 0)


def sum_at_owner(array, axis, dim):
    parts = in_blocks(array, dim, lax.axis_size(axis))
    arrived = lax.all_to_all(parts, axis, split_axis=0, concat_axis=0, tiled=True)
    return arrived.astype(jnp.float32).sum(axis=0)


def copy_for_each(array, axis):
    peers = lax.axis_size(axis)
    return lax.all_to_all(
        jnp.broadcast_to(array[None], (peers, *array.shape)), axis, 0, 0, tiled=True
    )


def laid_out(parts, dim):
    parts = jnp.moveaxis(parts, 0, dim)
    dims = parts.shape
    return parts.reshape(*dims[:dim], dims[dim] * dims[dim + 1], *dims[dim + 2 :])


def gathered_copies(array, axis, dim):
    parts = copy_for_each(array, axis)
    return laid_out(parts, dim)


def padded_to(lines, peers):
    spare = -len(lines) % peers
    return jnp.pad(lines, [(0, spare)] + [(0, 0)] * (lines.ndim - 1))


def sum_by_parts(array, axis):
    lines = array.reshape(-1, *array.shape[1:][-1:])
    own = lax.psum_scatter(
        padded_to(lines, lax.axis_size(axis)), axis, scatter_dimension=0, tiled=True
    )
    whole = lax.all_gather(own, axis).reshape(-1, *lines.shape[1:])
    return lax.slice_in_dim(whole, 0, len(lines)).reshape(array.shape)


def shifted(block, axis, distance):
    devices = range(lax.axis_size(axis))
    route = [(i - distance, i) for i in devices if i - distance in devices]
    return lax.ppermute(block, axis, route)


def orthonormal(summed):
    gram = jnp.einsum("kb,lb->kl", summed, summed, precision=lax.Precision.HIGHEST)
    chol = jnp.linalg.cholesky(gram)
    return jax.scipy.linalg.solve_triangular(chol, summed, lower=True).astype(jnp.bfloat16)


def local(panel, diag_tiles, dinv, u_fac, v_fac, ranks, sketch):
    left_factor = u_fac[0, :, 0]
    right_factor = v_fac[0, :, 0]
    slots = lax.broadcasted_iota(jnp.int32, (1, left_factor.shape[1], 1), 1)
    keep = slots < ranks[0, :, 0][:, None, None]
    random_probe = jnp.einsum(
        "jef,yf->jey", right_factor, sketch[0], preferred_element_type=jnp.float32
    )
    random_probe = jnp.where(keep, random_probe, 0.0).astype(jnp.bfloat16)
    range_component = jnp.einsum(
        "zgj,zgp->zpj", left_factor, random_probe, preferred_element_type=jnp.float32
    )
    share = sum_at_owner(range_component.astype(jnp.bfloat16), "upd", 0)
    range_basis = gathered_copies(jax.vmap(orthonormal)(share), "upd", 0)
    coefficient_matrix = jnp.einsum(
        "wxj,wuj->wxu", left_factor, range_basis, preferred_element_type=jnp.float32
    )
    coefficient_matrix = jnp.where(keep, coefficient_matrix, 0.0).astype(jnp.bfloat16)
    cross_term_part = jnp.einsum(
        "zgj,zgp->zpj", right_factor, coefficient_matrix, preferred_element_type=jnp.float32
    )
    cross_term = (
        sum_by_parts(cross_term_part.astype(jnp.bfloat16), "upd")
        .astype(jnp.float32)
        .astype(jnp.bfloat16)
    )
    rows_dev = panel.shape[2]
    first_row = lax.axis_index("upd") * rows_dev
    range_basis_rows = lax.dynamic_slice_in_dim(range_basis, first_row, rows_dev, 2)
    approximation = jnp.einsum(
        "fei,fej->fij", range_basis_rows, cross_term, preferred_element_type=jnp.float32
    )
    updated_tile = (panel[0].astype(jnp.float32) - approximation).astype(jnp.bfloat16)
    lowrank_factor = jnp.einsum(
        "vxn,en->vxe", updated_tile, dinv[0], preferred_element_type=jnp.float32
    ).astype(jnp.bfloat16)
    band = lowrank_factor.shape[0]
    received = jnp.stack(
        [shifted(lowrank_factor[offset - 1], "col", offset) for offset in range(1, band + 1)]
    )
    columns = lax.all_to_all(received, "upd", split_axis=2, concat_axis=1, tiled=True)
    total = sum_at_owner(
        (-jnp.einsum("mrc,mnc->rn", columns, columns, preferred_element_type=jnp.float32)).astype(
            jnp.bfloat16
        ),
        "upd",
        0,
    )
    diag_out = (diag_tiles[0].astype(jnp.float32) + total)[None]
    return (lowrank_factor[None], diag_out)


def solution(mesh):
    in_specs = (
        P("col", None, "upd", None),
        P("col", "upd", None),
        P("col", None, None),
        P("col", None, "upd", None, None),
        P("col", None, "upd", None, None),
        P("col", None, "upd"),
        P("col", None, None),
    )
    out_specs = (P("col", None, "upd", None), P("col", "upd", None))
    return jax.shard_map(local, mesh=mesh, in_specs=in_specs, out_specs=out_specs, check_vma=False)
```

profile of v0, /device:TPU:160, one launch (start us, length us, event | category | flops | bytes accessed | tf_op | source)
XLA Modules:
  0.0 297.2 jit_solution(5002424032824517877)
XLA Ops:
  7.2 0.9 iota_compare_fusion.2
  8.1 2.9 fusion.21
  11.0 20.1 %all_to_all.33 = bf16[8,1,64,1024]{3,2,1,0:T(8,128)(2,1)S(1)} all-to-all(bf16[8,1,64,1024]{3,2,1,0:T(8,128)(2,1)S(1)} %fusion.21), channel_id=1, replica_groups=mesh['upd'=8,'col'=32] {'upd'}, dimensions={0} | all-to-all | bytes 2097152 | tf_op jit(solution)/shard_map/all_to_all | solution.py:15
  31.7 5.8 %custom-call.8 = f32[1,64,64]{2,1,0:T(8,128)S(1)} custom-call(f32[1,64,64]{2,1,0:T(8,128)S(1)} %fusion.53), custom_call_target="Cholesky" | custom-call | tf_op jit(solution)/shard_map/vmap(jit(cholesky))/cholesky | solution.py:59
  38.9 4.9 %custom-call.9 = f32[1,1,64,64]{2,3,1,0:T(8,128)S(1)} custom-call(f32[1,1,64,64]{3,2,1,0:T(8,128)S(1)} %fusion.52), custom_call_target="InvertDiagBlocksLowerTriangular" | custom-call | tf_op jit(solution)/shard_map/vmap(jit(_solve_triangular))/triangular_solve | solution.py:60
  44.4 18.4 %all_to_all.34 = bf16[8,1,64,1024]{3,2,1,0:T(8,128)(2,1)S(1)} all-to-all(bf16[8,1,64,1024]{3,2,1,0:T(8,128)(2,1)S(1)} %broadcast_in_dim.36), channel_id=1, replica_groups=mesh['upd'=8,'col'=32] {'upd'}, dimensions={0} | all-to-all | bytes 2097152 | tf_op jit(solution)/shard_map/all_to_all | solution.py:21
  62.8 3.8 %fusion.15 = bf16[8,64,1024]{2,1,0:T(8,128)(2,1)} fusion(bf16[1,8,1,96,1024]{4,3,2,1,0:T(8,128)(2,1)} %param.11, bf16[1,8,1,96,1024]{4,3,2,1,0:T(8,128)(2,1)} %param.10, bf16[8,1,64,1024]{3,2,1,0:T(8,128)(2,1)S(1)} %all_to_all.34, pred[8,96]{1,0:T(8,128)(4,1)S(1)} %iota_compare_fusion.2), kind=kOutput, calls=%fused_computation.17 | convolution fusion | flops 201949184 | bytes 5243648 | tf_op jit(solution)/shard_map/zgj,zgp->zpj/dot_general | solution.py:81
  66.7 34.1 %reduce-scatter.2.cloned.1.call-done = bf16[64,1024]{1,0:T(8,128)(2,1)} async-done(((bf16[512,1024]{1,0:T(8,128)(2,1)}), bf16[64,1024]{1,0:T(8,128)(2,1)}) %reduce-scatter.2.cloned.1.call-update) | async-done | bytes 131088 | tf_op jit(solution)/shard_map/reduce_scatter | solution.py:44
  100.8 26.5 %all-gather.3.cloned.1.call-done = bf16[512,1024]{1,0:T(8,128)(2,1)} async-done(((bf16[64,1024]{1,0:T(8,128)(2,1)}), bf16[512,1024]{1,0:T(8,128)(2,1)}) %all-gather.3.cloned.1.call-update) | async-done | bytes 1048592 | tf_op jit(solution)/shard_map/all_gather | solution.py:47
  127.3 6.2 %fusion.4 = bf16[8,128,1024]{2,1,0:T(8,128)(2,1)} fusion(bf16[1,1024,1024]{2,1,0:T(8,128)(2,1)S(1)} %copy-done, bf16[8,64,1024]{2,1,0:T(8,128)(2,1)} %bitcast.126, bf16[1,8,128,1024]{3,2,1,0:T(8,128)(2,1)} %param.7, bf16[8,1,64,1024]{3,2,1,0:T(8,128)(2,1)S(1)} %all_to_all.34, s32[]{:T(128)S(6)} %select_n.17), kind=kOutput, calls=%fused_computation.8 | convolution fusion | flops 2285895680 | bytes 7471108 | tf_op jit(solution)/shard_map/vxn,en->vxe/dot_general | solution.py:96
  133.6 1.7 slice_bitcast_fusion
  135.3 3.4 %collective-permute-start = (bf16[128,1024]{1,0:T(8,128)(2,1)S(1)}, bf16[128,1024]{1,0:T(8,128)(2,1)S(1)}, u32[]{:S(2)}, u32[]{:S(2)}) collective-permute-start(bf16[128,1024]{1,0:T(8,128)(2,1)S(1)} %get-tuple-element.9), channel_id=1, source_target_pairs={{0,1},{1,2},{2,3},{3,4},{4,5},{5,6},{6,7},{7,8},{8,9},{9,10},{10,1... | collective-permute-start | bytes 786440 | tf_op jit(solution)/shard_map/ppermute | solution.py:54
  138.7 4.6 %collective-permute-start.1 = (bf16[128,1024]{1,0:T(8,128)(2,1)S(1)}, bf16[128,1024]{1,0:T(8,128)(2,1)S(1)}, u32[]{:S(2)}, u32[]{:S(2)}) collective-permute-start(bf16[128,1024]{1,0:T(8,128)(2,1)S(1)} %get-tuple-element.8), channel_id=1, source_target_pairs={{0,2},{1,3},{2,4},{3,5},{4,6},{5,7},{6,8},{7,9},{8,10},{9,11},{10,... | collective-permute-start | bytes 786440 | tf_op jit(solution)/shard_map/ppermute | solution.py:54
  143.3 2.7 collective-permute-start.7
  146.0 2.2 collective-permute-start.6
  148.2 1.9 collective-permute-start.5
  150.2 4.9 %collective-permute-start.2 = (bf16[128,1024]{1,0:T(8,128)(2,1)S(1)}, bf16[128,1024]{1,0:T(8,128)(2,1)S(1)}, u32[]{:S(2)}, u32[]{:S(2)}) collective-permute-start(bf16[128,1024]{1,0:T(8,128)(2,1)S(1)} %get-tuple-element.7), channel_id=1, source_target_pairs={{0,3},{1,4},{2,5},{3,6},{4,7},{5,8},{6,9},{7,10},{8,11},{9,12},{10... | collective-permute-start | bytes 786440 | tf_op jit(solution)/shard_map/ppermute | solution.py:54
  155.1 0.7 bitcast_dynamic-update-slice_fusion.7
  155.8 2.6 collective-permute-start.3
  159.1 22.9 %collective-permute-done.2 = bf16[128,1024]{1,0:T(8,128)(2,1)S(1)} collective-permute-done((bf16[128,1024]{1,0:T(8,128)(2,1)S(1)}, bf16[128,1024]{1,0:T(8,128)(2,1)S(1)}, u32[]{:S(2)}, u32[]{:S(2)}) %collective-permute-start.2) | collective-permute-done | bytes 262176 | tf_op jit(solution)/shard_map/ppermute | solution.py:54
  182.1 13.4 %collective-permute-start.4 = (bf16[128,1024]{1,0:T(8,128)(2,1)S(1)}, bf16[128,1024]{1,0:T(8,128)(2,1)S(1)}, u32[]{:S(2)}, u32[]{:S(2)}) collective-permute-start(bf16[128,1024]{1,0:T(8,128)(2,1)S(1)} %get-tuple-element.5), channel_id=1, source_target_pairs={{0,5},{1,6},{2,7},{3,8},{4,9},{5,10},{6,11},{7,12},{8,13},{9,14},{... | collective-permute-start | bytes 786440 | tf_op jit(solution)/shard_map/ppermute | solution.py:54
  195.5 0.7 bitcast_dynamic-update-slice_fusion.5
  196.2 0.7 bitcast_dynamic-update-slice_fusion.4
  197.0 14.6 %collective-permute-done.4 = bf16[128,1024]{1,0:T(8,128)(2,1)S(1)} collective-permute-done((bf16[128,1024]{1,0:T(8,128)(2,1)S(1)}, bf16[128,1024]{1,0:T(8,128)(2,1)S(1)}, u32[]{:S(2)}, u32[]{:S(2)}) %collective-permute-start.4) | collective-permute-done | bytes 262176 | tf_op jit(solution)/shard_map/ppermute | solution.py:54
  212.3 0.7 bitcast_dynamic-update-slice_fusion.2
  213.8 0.7 bitcast_dynamic-update-slice_fusion
  214.5 4.2 %copy.15 = bf16[8,128,1024]{1,0,2:T(8,128)(2,1)} copy(bf16[8,128,1024]{2,1,0:T(8,128)(2,1)} %bitcast_dynamic-update-slice_fusion) | data formatting | bytes 4194304 | tf_op jit(solution)/shard_map/stack | solution.py:100
  218.7 31.6 %all_to_all.35 = bf16[8,128,1024]{1,0,2:T(8,128)(2,1)} all-to-all(bf16[8,128,1024]{1,0,2:T(8,128)(2,1)} %copy.15), channel_id=1, replica_groups=mesh['upd'=8,'col'=32] {'upd'}, dimensions={2} | all-to-all | bytes 4194304 | tf_op jit(solution)/shard_map/all_to_all | solution.py:103
  250.2 4.1 %copy.16 = bf16[8,128,8,128]{3,1,2,0:T(8,128)(2,1)} copy(bf16[8,128,8,128]{1,0,3,2:T(8,128)(2,1)} %bitcast.120) | data formatting | bytes 4194304 | tf_op jit(solution)/shard_map/all_to_all | solution.py:103
  254.4 4.6 %fusion.1 = bf16[1024,1024]{1,0:T(8,128)(2,1)S(1)} fusion(bf16[8,1024,128]{2,1,0:T(8,128)(2,1)} %bitcast.123), kind=kOutput, calls=%fused_computation.3 | convolution fusion | flops 2149580800 | bytes 4194304 | tf_op jit(solution)/shard_map/mrc,mnc->rn/dot_general | solution.py:105
  258.9 29.7 %all_to_all.36 = bf16[8,128,1024]{2,1,0:T(8,128)(2,1)S(1)} all-to-all(bf16[8,128,1024]{2,1,0:T(8,128)(2,1)S(1)} %bitcast.124), channel_id=1, replica_groups=mesh['upd'=8,'col'=32] {'upd'}, dimensions={0} | all-to-all | bytes 4194304 | tf_op jit(solution)/shard_map/all_to_all | solution.py:15
  289.6 0.8 bitcast_add_fusion
  (27 shorter events, 5.8 us)
Async XLA Ops:
  7.2 120.2 %copy-start = (bf16[1,1024,1024]{2,1,0:T(8,128)(2,1)S(1)}, bf16[1,1024,1024]{2,1,0:T(8,128)(2,1)}, u32[]{:S(2)}) copy-start(bf16[1,1024,1024]{2,1,0:T(8,128)(2,1)} %param.9) | copy-start | bytes 6291460
  7.2 93.6 %reduce-scatter.2.cloned.1.call-start = ((), (), s32[]{:S(2)}) async-start(), calls=%async_computation.5 | async-start | bytes 1179648 | tf_op jit(solution)/shard_map/reduce_scatter | solution.py:44
  66.6 60.7 %all-gather.3.cloned.1.call-start = ((), (), s32[]{:S(2)}) async-start(), calls=%async_computation.6 | async-start | bytes 1179648 | tf_op jit(solution)/shard_map/all_gather | solution.py:47
  135.3 14.9 %collective-permute-start = (bf16[128,1024]{1,0:T(8,128)(2,1)S(1)}, bf16[128,1024]{1,0:T(8,128)(2,1)S(1)}, u32[]{:S(2)}, u32[]{:S(2)}) collective-permute-start(bf16[128,1024]{1,0:T(8,128)(2,1)S(1)} %get-tuple-element.9), channel_id=1, source_target_pairs={{0,1},{1,2},{2,3},{3,4},{4,5},{5,6},{6,7},{7,8},{8,9},{9,10},{10,1... | collective-permute-start | bytes 786440 | tf_op jit(solution)/shard_map/ppermute | solution.py:54
  138.7 17.1 %collective-permute-start.1 = (bf16[128,1024]{1,0:T(8,128)(2,1)S(1)}, bf16[128,1024]{1,0:T(8,128)(2,1)S(1)}, u32[]{:S(2)}, u32[]{:S(2)}) collective-permute-start(bf16[128,1024]{1,0:T(8,128)(2,1)S(1)} %get-tuple-element.8), channel_id=1, source_target_pairs={{0,2},{1,3},{2,4},{3,5},{4,6},{5,7},{6,8},{7,9},{8,10},{9,11},{10,... | collective-permute-start | bytes 786440 | tf_op jit(solution)/shard_map/ppermute | solution.py:54
  143.3 70.4 %collective-permute-start.7 = (bf16[128,1024]{1,0:T(8,128)(2,1)S(1)}, bf16[128,1024]{1,0:T(8,128)(2,1)S(1)}, u32[]{:S(2)}, u32[]{:S(2)}) collective-permute-start(bf16[128,1024]{1,0:T(8,128)(2,1)S(1)} %get-tuple-element.2), channel_id=1, source_target_pairs={{0,8},{1,9},{2,10},{3,11},{4,12},{5,13},{6,14},{7,15},{8,16},{9,17... | collective-permute-start | bytes 786440 | tf_op jit(solution)/shard_map/ppermute | solution.py:54
  146.0 67.1 %collective-permute-start.6 = (bf16[128,1024]{1,0:T(8,128)(2,1)S(1)}, bf16[128,1024]{1,0:T(8,128)(2,1)S(1)}, u32[]{:S(2)}, u32[]{:S(2)}) collective-permute-start(bf16[128,1024]{1,0:T(8,128)(2,1)S(1)} %get-tuple-element.3), channel_id=1, source_target_pairs={{0,7},{1,8},{2,9},{3,10},{4,11},{5,12},{6,13},{7,14},{8,15},{9,16}... | collective-permute-start | bytes 786440 | tf_op jit(solution)/shard_map/ppermute | solution.py:54
  148.2 64.1 %collective-permute-start.5 = (bf16[128,1024]{1,0:T(8,128)(2,1)S(1)}, bf16[128,1024]{1,0:T(8,128)(2,1)S(1)}, u32[]{:S(2)}, u32[]{:S(2)}) collective-permute-start(bf16[128,1024]{1,0:T(8,128)(2,1)S(1)} %get-tuple-element.4), channel_id=1, source_target_pairs={{0,6},{1,7},{2,8},{3,9},{4,10},{5,11},{6,12},{7,13},{8,14},{9,15},... | collective-permute-start | bytes 786440 | tf_op jit(solution)/shard_map/ppermute | solution.py:54
  150.2 31.8 %collective-permute-start.2 = (bf16[128,1024]{1,0:T(8,128)(2,1)S(1)}, bf16[128,1024]{1,0:T(8,128)(2,1)S(1)}, u32[]{:S(2)}, u32[]{:S(2)}) collective-permute-start(bf16[128,1024]{1,0:T(8,128)(2,1)S(1)} %get-tuple-element.7), channel_id=1, source_target_pairs={{0,3},{1,4},{2,5},{3,6},{4,7},{5,8},{6,9},{7,10},{8,11},{9,12},{10... | collective-permute-start | bytes 786440 | tf_op jit(solution)/shard_map/ppermute | solution.py:54
  155.8 40.4 %collective-permute-start.3 = (bf16[128,1024]{1,0:T(8,128)(2,1)S(1)}, bf16[128,1024]{1,0:T(8,128)(2,1)S(1)}, u32[]{:S(2)}, u32[]{:S(2)}) collective-permute-start(bf16[128,1024]{1,0:T(8,128)(2,1)S(1)} %get-tuple-element.6), channel_id=1, source_target_pairs={{0,4},{1,5},{2,6},{3,7},{4,8},{5,9},{6,10},{7,11},{8,12},{9,13},{1... | collective-permute-start | bytes 786440 | tf_op jit(solution)/shard_map/ppermute | solution.py:54
  182.1 29.5 %collective-permute-start.4 = (bf16[128,1024]{1,0:T(8,128)(2,1)S(1)}, bf16[128,1024]{1,0:T(8,128)(2,1)S(1)}, u32[]{:S(2)}, u32[]{:S(2)}) collective-permute-start(bf16[128,1024]{1,0:T(8,128)(2,1)S(1)} %get-tuple-element.5), channel_id=1, source_target_pairs={{0,5},{1,6},{2,7},{3,8},{4,9},{5,10},{6,11},{7,12},{8,13},{9,14},{... | collective-permute-start | bytes 786440 | tf_op jit(solution)/shard_map/ppermute | solution.py:54
  288.6 1.0 copy-start.1
Sparse Core Ops, SparseCore 0:
  66.8 33.9 reduce-scatter.1
  102.7 24.6 all-gather.2
where the time goes:
time: 298 us; the launch traced here: 297 us
  blocking collectives  99.7 us (33%)
  waiting for transfers between devices  98.3 us (33%)
  starting transfers between devices  35.7 us (12%)
  matrix products  18.4 us (6%)
  local copies, waits for them, and re-layouts  16.6 us (6%)
  other arithmetic  14.3 us (5%)
  between operations  14.2 us (5%)
    all_to_all x2, blocking collectives, sum_at_owner(): lax.all_to_all(parts, axis, split_axis=0, concat_axis=0, tiled=True)  49.7 us
    ppermute x8, waiting for transfers between devices, shifted(): return lax.ppermute(block, axis, route)  37.7 us
    ppermute x8, starting transfers between devices, shifted(): return lax.ppermute(block, axis, route)  35.6 us
    reduce_scatter x1, waiting for transfers between devices, sum_by_parts(): lax.psum_scatter(padded_to(lines, lax.axis_size(axis)), axis, scatter_dim...  34.1 us
    all_to_all x1, blocking collectives, local(): lax.all_to_all(received, 'upd', split_axis=2, concat_axis=1, tiled=True)  31.6 us
    all_gather x1, waiting for transfers between devices, sum_by_parts(): whole = lax.all_gather(own, axis).reshape(-1, *lines.shape[1:])  26.5 us
    all_to_all x1, blocking collectives, copy_for_each(): lax.all_to_all(jnp.broadcast_to(array[None], (peers, *array.shape)), axis...  18.4 us
    another operation x3, other arithmetic, orthonormal(): chol = jnp.linalg.cholesky(gram)  6.52 us
  transfers between devices with their start and end apart: 10, of which 5 were waited for; matrix products, arithmetic and copies ran while one was open for 2% of the time, Pallas kernels for 0%

commit v1 on v0

v1 whole, which is shorter than its diff:
```python
import jax
import jax.numpy as jnp
from jax import lax
from jax.experimental import pallas as pl
from jax.experimental.pallas import tpu as pltpu
from jax.sharding import PartitionSpec as P

F32 = jnp.float32
BF16 = jnp.bfloat16
AXES = ("upd", "col")
NU = 8
NX = 4
NC = 32
HALF = 5
BLK = 128


def dot(a, b, dims, precision=None):
    return lax.dot_general(a, b, (dims, ((), ())), precision=precision, preferred_element_type=F32)


def perm(block, route):
    pairs = []
    for u in range(NU):
        for c in range(NC):
            to = route(u, c)
            if to is not None:
                pairs.append((u * NC + c, to[0] * NC + to[1]))
    return lax.ppermute(block, AXES, pairs)


def along_x(k):
    return lambda u, c: ((u + 2 * k) % NU, c)


def along_upd(k):
    return lambda u, c: ((u + k) % NU, c)


def partner(u, c):
    return (u ^ 1, c)


def to_owner(k):
    def route(u, c):
        j = c + u + 1
        return None if j >= NC else ((u + k) % NU, j)

    return route


def sketch_kernel(where, ranks, v_ref, u_ref, sketch_ref, send_ref, keep_ref):
    k = pl.program_id(0)
    core = where[1]
    pair = (where[0] + k) % NX
    for side in range(2):
        which = core if side else 1 - core
        probe = dot(v_ref[which], sketch_ref[...], ((1,), (1,)))
        slots = lax.broadcasted_iota(jnp.int32, probe.shape, 0)
        probe = jnp.where(slots < ranks[2 * pair + which], probe, 0.0).astype(BF16)
        out = dot(probe, u_ref[which], ((0,), (0,)))
        if side:
            keep_ref[0] = out
        else:
            send_ref[0] = out.astype(BF16)


def sketch_call(where, ranks, v, u, sketch):
    tiles, slots, width = v.shape
    rk = sketch.shape[0]
    pairs = pl.BlockSpec((2, slots, width), lambda k, w, r: ((w[0] + k) % NX, 0, 0))
    return pl.pallas_call(
        sketch_kernel,
        out_shape=(
            jax.ShapeDtypeStruct((NX, rk, width), BF16),
            jax.ShapeDtypeStruct((NX, rk, width), F32),
        ),
        grid_spec=pltpu.PrefetchScalarGridSpec(
            num_scalar_prefetch=2,
            grid=(NX,),
            in_specs=[pairs, pairs, pl.BlockSpec((rk, width), lambda k, w, r: (0, 0))],
            out_specs=[
                pl.BlockSpec((1, rk, width), lambda k, w, r: (k, 0, 0)),
                pl.BlockSpec((1, rk, width), lambda k, w, r: (k, 0, 0)),
            ],
        ),
        name="sketch_product",
    )(where, ranks, v, u, sketch)


def project_kernel(where, ranks, u_ref, v_ref, *refs):
    bases, (send_ref, keep_ref) = refs[:NU], refs[NU:]
    d = pl.program_id(0)
    core = where[1]
    pair = (where[0] + NX - d) % NX
    for step in range(NX):

        @pl.when(d == step)
        def _(step=step):
            for side in range(2):
                which = core if side else 1 - core
                basis = bases[step if side else NX + step][...]
                coeff = dot(u_ref[which], basis, ((1,), (1,)))
                slots = lax.broadcasted_iota(jnp.int32, coeff.shape, 0)
                coeff = jnp.where(slots < ranks[2 * pair + which], coeff, 0.0).astype(BF16)
                out = dot(coeff, v_ref[which], ((0,), (0,)))
                if side:
                    keep_ref[0] = out
                else:
                    send_ref[0] = out.astype(BF16)


def project_call(where, ranks, u, v, bases):
    tiles, slots, width = v.shape
    rk = bases[0].shape[0]
    pairs = pl.BlockSpec((2, slots, width), lambda d, w, r: ((w[0] + NX - d) % NX, 0, 0))
    whole = pl.BlockSpec((rk, width), lambda d, w, r: (0, 0))
    out = pl.BlockSpec((1, rk, width), lambda d, w, r: ((NX - d) % NX, 0, 0))
    return pl.pallas_call(
        project_kernel,
        out_shape=(
            jax.ShapeDtypeStruct((NX, rk, width), BF16),
            jax.ShapeDtypeStruct((NX, rk, width), F32),
        ),
        grid_spec=pltpu.PrefetchScalarGridSpec(
            num_scalar_prefetch=2,
            grid=(NX,),
            in_specs=[pairs, pairs] + [whole] * NU,
            out_specs=[out, out],
        ),
        name="basis_product",
    )(where, ranks, u, v, *bases)


def pair_sum_kernel(keep_ref, got_ref, own_ref, a_ref, b_ref, c_ref):
    for k, ref in enumerate((own_ref, a_ref, b_ref, c_ref)):
        ref[...] = (keep_ref[k] + got_ref[k].astype(F32)).astype(ref.dtype)


def pair_sum(keep, got):
    shape = keep.shape[1:]
    return pl.pallas_call(
        pair_sum_kernel,
        out_shape=(jax.ShapeDtypeStruct(shape, F32),)
        + tuple(jax.ShapeDtypeStruct(shape, BF16) for _ in range(3)),
        name="pair_sum",
    )(keep, got)


def owner_parts(send, keep):
    got = perm(send, partner)
    own, *others = pair_sum(keep, got)
    return [own] + [perm(part, along_x(k + 1)) for k, part in enumerate(others)]


def basis_kernel(own_ref, a_ref, b_ref, c_ref, basis_ref):
    summed = own_ref[...] + a_ref[...].astype(F32) + b_ref[...].astype(F32) + c_ref[...].astype(F32)
    rk = summed.shape[0]
    gram = dot(summed, summed, ((1,), (1,)), lax.Precision.HIGHEST)
    rows = lax.broadcasted_iota(jnp.int32, (rk, rk), 0)
    cols = lax.broadcasted_iota(jnp.int32, (rk, rk), 1)
    row_at = lax.broadcasted_iota(jnp.int32, (rk, 1), 0)
    work = jnp.concatenate([gram, jnp.where(rows == cols, 1.0, 0.0)], axis=1)
    for k in range(rk):
        row = work[k : k + 1, :]
        scaled = row * (1.0 / work[k : k + 1, k : k + 1])
        col = jnp.where(row_at > k, work[:, k : k + 1], 0.0)
        work = work - col * scaled
    pivots = jnp.sum(jnp.where(rows == cols, work[:, :rk], 0.0), axis=1, keepdims=True)
    inverse = work[:, rk:] * lax.rsqrt(pivots)
    basis_ref[...] = dot(inverse, summed, ((1,), (0,)), lax.Precision.HIGHEST).astype(BF16)


def basis_call(parts):
    return pl.pallas_call(
        basis_kernel, out_shape=jax.ShapeDtypeStruct(parts[0].shape, BF16), name="orthonormal"
    )(*parts)


def gathered(own):
    mine = [own] + [perm(own, along_x(d)) for d in range(1, NX)]
    return mine + [perm(block, partner) for block in mine]


def split_kernel(where, panel_ref, *refs):
    outs, sems = refs[:-1], refs[-1]
    copies = []
    for k, out in enumerate(outs):
        copies.append(
            pltpu.make_async_copy(panel_ref.at[(where[2] + k) % NU], out, sems.at[k])
        )
    for copy in copies:
        copy.start()
    for copy in copies:
        copy.wait()


def split_panel(where, panel):
    shape = panel.shape[1:]
    anywhere = pl.BlockSpec(memory_space=pl.ANY)
    return pl.pallas_call(
        split_kernel,
        out_shape=tuple(jax.ShapeDtypeStruct(shape, BF16) for _ in range(NU)),
        in_specs=[pl.BlockSpec(memory_space=pltpu.SMEM), anywhere],
        out_specs=[anywhere] * NU,
        scratch_shapes=[pltpu.SemaphoreType.DMA((NU,))],
        name="split_panel",
    )(where, panel)


def tile_kernel(where, basis_ref, own_ref, a_ref, b_ref, c_ref, dinv_ref, *refs):
    rows = refs[:NU]
    cross_ref, outs, solved = refs[NU], refs[NU + 1 : NU + 1 + NU], refs[-1]
    cross = own_ref[...] + a_ref[...].astype(F32) + b_ref[...].astype(F32) + c_ref[...].astype(F32)
    cross = cross.astype(BF16)
    cross_ref[...] = cross
    dinv = dinv_ref[...]
    for k in range(NU):
        at = pl.multiple_of(((where[2] + NU - k) % NU) * BLK, BLK)
        part = basis_ref[:, pl.ds(at, BLK)]
        updated = (rows[k][...].astype(F32) - dot(part, cross, ((0,), (0,)))).astype(BF16)
        solved[k * BLK : (k + 1) * BLK] = dot(updated, dinv, ((1,), (1,))).astype(BF16)
    for k in range(HALF - 1):
        solved[(NU + k) * BLK : (NU + k + 1) * BLK] = solved[k * BLK : (k + 1) * BLK]
    for s in range(NU):
        k = (NU - s) % NU
        outs[s][...] = dot(
            solved[k * BLK : (k + 1) * BLK], solved[k * BLK : (k + HALF) * BLK], ((1,), (1,))
        ).astype(BF16)


def tile_call(where, basis, parts, dinv, rows):
    rk, width = basis.shape
    vmem = pl.BlockSpec(memory_space=pltpu.VMEM)
    return pl.pallas_call(
        tile_kernel,
        out_shape=(jax.ShapeDtypeStruct((rk, width), BF16),)
        + tuple(jax.ShapeDtypeStruct((BLK, HALF * BLK), BF16) for _ in range(NU)),
        in_specs=[pl.BlockSpec(memory_space=pltpu.SMEM)] + [vmem] * (6 + NU),
        out_specs=[vmem] * (1 + NU),
        scratch_shapes=[pltpu.VMEM(((NU + HALF - 1) * BLK, width), BF16)],
        name="tile_product",
    )(where, basis, *parts, dinv, *rows)


def rows_kernel(where, panel_ref, dinv_ref, *refs):
    bases, crosses, out_ref = refs[:NU], refs[NU : 2 * NU], refs[-1]
    d = pl.program_id(0)
    core = where[1]
    at = pl.multiple_of(where[2] * BLK, BLK)
    for step in range(NX):

        @pl.when(d == step)
        def _(step=step):
            for side in range(2):
                which = core if side else 1 - core
                source = step if side else NX + step
                part = bases[source][:, pl.ds(at, BLK)]
                lowrank = dot(part, crosses[source][...], ((0,), (0,)))
                updated = (panel_ref[which].astype(F32) - lowrank).astype(BF16)
                out_ref[which] = dot(updated, dinv_ref[...], ((1,), (1,))).astype(BF16)


def rows_call(where, panel, dinv, bases, crosses):
    rk, width = bases[0].shape
    pairs = pl.BlockSpec((2,) + panel.shape[1:], lambda d, w: ((w[0] + NX - d) % NX, 0, 0))
    whole = pl.BlockSpec((rk, width), lambda d, w: (0, 0))
    return pl.pallas_call(
        rows_kernel,
        out_shape=jax.ShapeDtypeStruct(panel.shape, BF16),
        grid_spec=pltpu.PrefetchScalarGridSpec(
            num_scalar_prefetch=1,
            grid=(NX,),
            in_specs=[pairs, pl.BlockSpec(dinv.shape, lambda d, w: (0, 0))] + [whole] * (2 * NU),
            out_specs=pairs,
        ),
        name="panel_rows",
    )(where, panel, dinv, *bases, *crosses)


def collect_kernel(*refs):
    got, (total_ref, a_ref, b_ref, c_ref) = refs[:NU], refs[NU:]
    total = got[0][...].astype(F32)
    for block in got[1:]:
        total = total + block[...].astype(F32)
    total_ref[...] = total
    for d, ref in ((1, a_ref), (2, b_ref), (3, c_ref)):
        ref[...] = total[:, d * BLK : (d + 1) * BLK].T


def collect_call(got):
    mirrored = jax.ShapeDtypeStruct((BLK, BLK), F32)
    return pl.pallas_call(
        collect_kernel,
        out_shape=(jax.ShapeDtypeStruct(got[0].shape, F32), mirrored, mirrored, mirrored),
        name="collect",
    )(*got)


def diag_kernel(where, diag_ref, total_ref, a_ref, b_ref, c_ref, out_ref):
    for d in range(HALF):
        at = pl.ds(pl.multiple_of(((where[2] + NU - d) % NU) * BLK, BLK), BLK)
        out_ref[:, at] = diag_ref[:, at].astype(F32) - total_ref[:, d * BLK : (d + 1) * BLK]
    for d, ref in ((1, a_ref), (2, b_ref), (3, c_ref)):
        at = pl.ds(pl.multiple_of(((where[2] + d) % NU) * BLK, BLK), BLK)
        out_ref[:, at] = diag_ref[:, at].astype(F32) - ref[...]


def diag_call(where, diag, total, mirrored):
    vmem = pl.BlockSpec(memory_space=pltpu.VMEM)
    return pl.pallas_call(
        diag_kernel,
        out_shape=jax.ShapeDtypeStruct(diag.shape, F32),
        in_specs=[pl.BlockSpec(memory_space=pltpu.SMEM)] + [vmem] * 5,
        out_specs=vmem,
        name="diagonal",
    )(where, diag, total, *mirrored)


def local(panel, diag_tiles, dinv, u_fac, v_fac, ranks, sketch):
    at = lax.axis_index("upd").astype(jnp.int32)
    where = jnp.stack([at // 2, at % 2, at])
    u, v, ranks = u_fac[0, :, 0], v_fac[0, :, 0], ranks[0, :, 0]

    parts = owner_parts(*sketch_call(where, ranks, v, u, sketch[0]))
    blocks = split_panel(where, panel[0])
    rows = [blocks[0]] + [perm(blocks[k], along_upd(k)) for k in range(1, NU)]
    basis = basis_call(parts)
    bases = gathered(basis)
    parts = owner_parts(*project_call(where, ranks, u, v, bases))
    cross, *products = tile_call(where, basis, parts, dinv[0], rows)
    got = [perm(block, to_owner(k)) for k, block in enumerate(products)]
    crosses = gathered(cross)
    panel_out = rows_call(where, panel[0], dinv[0], bases, crosses)
    total, *mirrored = collect_call(got)
    mirrored = [perm(block, along_upd(-d - 1)) for d, block in enumerate(mirrored)]
    diag_out = diag_call(where, diag_tiles[0], total, mirrored)
    return (panel_out[None], diag_out[None])


def solution(mesh):
    in_specs = (
        P("col", None, "upd", None),
        P("col", "upd", None),
        P("col", None, None),
        P("col", None, "upd", None, None),
        P("col", None, "upd", None, None),
        P("col", None, "upd"),
        P("col", None, None),
    )
    out_specs = (P("col", None, "upd", None), P("col", "upd", None))
    return jax.shard_map(local, mesh=mesh, in_specs=in_specs, out_specs=out_specs, check_vma=False)
```

time: 298 us -> 266 us (0.89); the launches traced: 297 us -> 261 us
  Pallas kernels: 0 us -> 119 us
  blocking collectives: 99.7 us -> 0 us
  waiting for transfers between devices: 98.3 us -> 48 us
  starting transfers between devices: 35.7 us -> 85.9 us
  matrix products: 18.4 us -> 0 us
  other arithmetic: 14.3 us -> 0.59 us
  between operations: 14.2 us -> 1.09 us
  local copies, waits for them, and re-layouts: 16.6 us -> 6.49 us
    pallas_call x0 -> x10, Pallas kernels: none -> 119 us  [the longest x1 65.4 us: split_panel(): pl.pallas_call(split_kernel, out_shape=tuple((jax.ShapeDtypeStruct(shape,...]
    all_to_all x4 -> x0, blocking collectives: 99.7 us -> none  [the longest x2 49.7 us: sum_at_owner(): lax.all_to_all(parts, axis, split_axis=0, concat_axis=0, tiled=True)]
    ppermute x8 -> x40, starting transfers between devices: 35.6 us -> 85.9 us  [perm(): return lax.ppermute(block, AXES, pairs)]
    reduce_scatter x1 -> x0, waiting for transfers between devices: 34.1 us -> none  [sum_by_parts(): lax.psum_scatter(padded_to(lines, lax.axis_size(axis)), axis, scatter_dim...]
    all_gather x1 -> x0, waiting for transfers between devices: 26.5 us -> none  [sum_by_parts(): whole = lax.all_gather(own, axis).reshape(-1, *lines.shape[1:])]
    dot_general x5 -> x0, matrix products: 17.9 us -> none  [the longest x1 6.22 us: local(): jnp.einsum('vxn,en->vxe', updated_tile, dinv[0], preferred_element_type=j...]
    another operation x5 -> x1, other arithmetic: 12.1 us -> 0.59 us  [local(): where = jnp.stack([at // 2, at % 2, at])]
    ppermute x8 -> x40, waiting for transfers between devices: 37.7 us -> 48 us  [perm(): return lax.ppermute(block, AXES, pairs)]
  transfers between devices with their start and end apart: 10 -> 40, of which waited for: 5 -> 16; matrix products, arithmetic and copies ran while one was open for 2% -> 0% of each run, Pallas kernels for 0% -> 28%
where the time goes in v1:
time: 266 us; the launch traced here: 261 us
  Pallas kernels  119 us (45%)
  starting transfers between devices  85.9 us (32%)
  waiting for transfers between devices  48 us (18%)
  local copies, waits for them, and re-layouts  6.49 us (2%)
    ppermute x40, starting transfers between devices, perm(): return lax.ppermute(block, AXES, pairs)  85.9 us
    pallas_call x1, Pallas kernels, split_panel(): pl.pallas_call(split_kernel, out_shape=tuple((jax.ShapeDtypeStruct(shape,...  65.4 us
    ppermute x40, waiting for transfers between devices, perm(): return lax.ppermute(block, AXES, pairs)  48 us
    pallas_call x1, Pallas kernels, tile_call(): pl.pallas_call(tile_kernel, out_shape=(jax.ShapeDtypeStruct((rk, width),...  12.5 us
    pallas_call x1, Pallas kernels, rows_call(): pl.pallas_call(rows_kernel, out_shape=jax.ShapeDtypeStruct(panel.shape, B...  10.9 us
    pallas_call x1, Pallas kernels, basis_call(): pl.pallas_call(basis_kernel, out_shape=jax.ShapeDtypeStruct(parts[0].shap...  8.29 us
    pallas_call x1, Pallas kernels, project_call(): pl.pallas_call(project_kernel, out_shape=(jax.ShapeDtypeStruct((NX, rk, w...  6.67 us
    unnamed x80, local copies, waits for them, and re-layouts  6.49 us
  transfers between devices with their start and end apart: 40, of which 16 were waited for; matrix products, arithmetic and copies ran while one was open for 0% of the time, Pallas kernels for 28%

profile of v1, /device:TPU:160, one launch (start us, length us, event | category | flops | bytes accessed | tf_op | source)
XLA Modules:
  0.0 260.9 jit_solution(7077740671933784761)
XLA Ops:
  1.2 6.2 %sketch_product.1 = (bf16[4,64,1024]{2,1,0:T(8,128)(2,1)}, f32[4,64,1024]{2,1,0:T(8,128)}) custom-call(s32[3]{0:T(128)} %pad_add_fusion.where, s32[8]{0:T(128)} %bitcast.24, bf16[8,96,1024]{2,1,0:T(8,128)(2,1)} %bitcast.16, bf16[8,96,1024]{2,1,0:T(8,128)(2,1)} %bitcast.18, bf16[64,1024]{1,0:T(8,128)(2,1)} %bitcast.23), custom_call_target="tpu_custom_call" | custom-call | tf_op jit(solution)/shard_map/sketch_product/pallas_call | solution.py:72
  10.4 2.3 pair_sum.2
  14.1 2.7 %collective-permute-start.2 = (bf16[64,1024]{1,0:T(8,128)(2,1)}, bf16[64,1024]{1,0:T(8,128)(2,1)S(1)}, u32[]{:S(2)}, u32[]{:S(2)}) collective-permute-start(bf16[64,1024]{1,0:T(8,128)(2,1)} %get-tuple-element.39), channel_id=1, source_target_pairs={{0,128},{1,129},{2,130},{3,131},{4,132},{5,133},{6,134},{7,135},{8... | collective-permute-start | bytes 393224 | tf_op jit(solution)/shard_map/ppermute | solution.py:29
  19.6 3.8 %collective-permute-done.2.b_ref = bf16[64,1024]{1,0:T(8,128)(2,1)S(1)} collective-permute-done((bf16[64,1024]{1,0:T(8,128)(2,1)}, bf16[64,1024]{1,0:T(8,128)(2,1)S(1)}, u32[]{:S(2)}, u32[]{:S(2)}) %collective-permute-start.2) | collective-permute-done | bytes 131104 | tf_op jit(solution)/shard_map/ppermute | solution.py:29
  24.1 8.3 %orthonormal.1.refs_0_.basis_ref = bf16[64,1024]{1,0:T(8,128)(2,1)} custom-call(f32[64,1024]{1,0:T(8,128)} %get-tuple-element.37.own_ref, bf16[64,1024]{1,0:T(8,128)(2,1)} %copy-done.34, bf16[64,1024]{1,0:T(8,128)(2,1)} %copy-done.35, bf16[64,1024]{1,0:T(8,128)(2,1)} %copy-done.36), custom_call_target="tpu_custom_call" | custom-call | tf_op jit(solution)/shard_map/orthonormal/pallas_call | solution.py:175
  34.6 2.4 collective-permute-start.5
  37.6 5.8 %collective-permute-done.4.refs_1_ = bf16[64,1024]{1,0:T(8,128)(2,1)S(1)} collective-permute-done((bf16[64,1024]{1,0:T(8,128)(2,1)}, bf16[64,1024]{1,0:T(8,128)(2,1)S(1)}, u32[]{:S(2)}, u32[]{:S(2)}) %collective-permute-start.4) | collective-permute-done | bytes 131104 | tf_op jit(solution)/shard_map/ppermute | solution.py:29
  46.1 6.7 %basis_product.1 = (bf16[4,64,1024]{2,1,0:T(8,128)(2,1)}, f32[4,64,1024]{2,1,0:T(8,128)}) custom-call(s32[3]{0:T(128)} %pad_add_fusion.where, s32[8]{0:T(128)} %bitcast.25, bf16[8,96,1024]{2,1,0:T(8,128)(2,1)} %bitcast.19, bf16[8,96,1024]{2,1,0:T(8,128)(2,1)} %bitcast.17, bf16[64,1024]{1,0:T(8,128)(2,1)} %orthonormal.1.refs_0_.basis_ref, ...), custom_call_target="tpu_custom_call" | custom-call | tf_op jit(solution)/shard_map/basis_product/pallas_call | solution.py:119
  52.9 65.4 %split_panel.1 = (bf16[128,1024]{1,0:T(8,128)(2,1)}, bf16[128,1024]{1,0:T(8,128)(2,1)}, bf16[128,1024]{1,0:T(8,128)(2,1)}, bf16[128,1024]{1,0:T(8,128)(2,1)}, bf...) custom-call(s32[3]{0:T(128)} %pad_add_fusion.where, ...), custom_call_target="tpu_custom_call" | custom-call | tf_op jit(solution)/shard_map/split_panel/pallas_call | solution.py:201
  119.6 3.3 %collective-permute-start.18 = (bf16[128,1024]{1,0:T(8,128)(2,1)}, bf16[128,1024]{1,0:T(8,128)(2,1)S(1)}, u32[]{:S(2)}, u32[]{:S(2)}) collective-permute-start(bf16[128,1024]{1,0:T(8,128)(2,1)} %get-tuple-element.51), channel_id=1, source_target_pairs={{0,128},{1,129},{2,130},{3,131},{4,132},{5,133},{6,134},{7,135},{8... | collective-permute-start | bytes 786440 | tf_op jit(solution)/shard_map/ppermute | solution.py:29
  122.9 4.4 %collective-permute-done.15.refs_1_ = bf16[128,1024]{1,0:T(8,128)(2,1)S(1)} collective-permute-done((bf16[128,1024]{1,0:T(8,128)(2,1)}, bf16[128,1024]{1,0:T(8,128)(2,1)S(1)}, u32[]{:S(2)}, u32[]{:S(2)}) %collective-permute-start.15) | collective-permute-done | bytes 262176 | tf_op jit(solution)/shard_map/ppermute | solution.py:29
  129.2 3.9 %collective-permute-start.21 = (bf16[128,1024]{1,0:T(8,128)(2,1)}, bf16[128,1024]{1,0:T(8,128)(2,1)S(1)}, u32[]{:S(2)}, u32[]{:S(2)}) collective-permute-start(bf16[128,1024]{1,0:T(8,128)(2,1)} %get-tuple-element.54), channel_id=1, source_target_pairs={{0,224},{1,225},{2,226},{3,227},{4,228},{5,229},{6,230},{7,231},{8... | collective-permute-start | bytes 786440 | tf_op jit(solution)/shard_map/ppermute | solution.py:29
  133.1 2.2 pair_sum.3
  137.4 9.9 %collective-permute-start.12 = (bf16[64,1024]{1,0:T(8,128)(2,1)}, bf16[64,1024]{1,0:T(8,128)(2,1)S(1)}, u32[]{:S(2)}, u32[]{:S(2)}) collective-permute-start(bf16[64,1024]{1,0:T(8,128)(2,1)} %get-tuple-element.44), channel_id=1, source_target_pairs={{0,64},{1,65},{2,66},{3,67},{4,68},{5,69},{6,70},{7,71},{8,72},{9,... | collective-permute-start | bytes 393224 | tf_op jit(solution)/shard_map/ppermute | solution.py:29
  149.2 2.5 collective-permute-start.14
  151.8 3.3 %collective-permute-done.13.b_ref = bf16[64,1024]{1,0:T(8,128)(2,1)S(1)} collective-permute-done((bf16[64,1024]{1,0:T(8,128)(2,1)}, bf16[64,1024]{1,0:T(8,128)(2,1)S(1)}, u32[]{:S(2)}, u32[]{:S(2)}) %collective-permute-start.13) | collective-permute-done | bytes 131104 | tf_op jit(solution)/shard_map/ppermute | solution.py:29
  155.1 2.4 collective-permute-done.14.c_ref
  158.1 12.5 %tile_product.1 = (bf16[64,1024]{1,0:T(8,128)(2,1)}, bf16[128,640]{1,0:T(8,128)(2,1)}, bf16[128,640]{1,0:T(8,128)(2,1)}, bf16[128,640]{1,0:T(8,128)(2,1)}, bf16[...) custom-call(s32[3]{0:T(128)} %pad_add_fusion.where, ...), custom_call_target="tpu_custom_call" | custom-call | tf_op jit(solution)/shard_map/tile_product/pallas_call | solution.py:235
  170.6 3.5 %collective-permute-start.29 = (bf16[128,640]{1,0:T(8,128)(2,1)}, bf16[128,640]{1,0:T(8,128)(2,1)S(1)}, u32[]{:S(2)}, u32[]{:S(2)}) collective-permute-start(bf16[128,640]{1,0:T(8,128)(2,1)} %get-tuple-element.56), channel_id=1, source_target_pairs={{0,1},{1,2},{2,3},{3,4},{4,5},{5,6},{6,7},{7,8},{8,9},{9,10},{10,1... | collective-permute-start | bytes 491528 | tf_op jit(solution)/shard_map/ppermute | solution.py:29
  174.1 3.0 %collective-permute-start.30 = (bf16[128,640]{1,0:T(8,128)(2,1)}, bf16[128,640]{1,0:T(8,128)(2,1)S(1)}, u32[]{:S(2)}, u32[]{:S(2)}) collective-permute-start(bf16[128,640]{1,0:T(8,128)(2,1)} %get-tuple-element.57), channel_id=1, source_target_pairs={{0,33},{1,34},{2,35},{3,36},{4,37},{5,38},{6,39},{7,40},{8,41},{9,... | collective-permute-start | bytes 491528 | tf_op jit(solution)/shard_map/ppermute | solution.py:29
  177.1 2.4 collective-permute-start.31
  179.5 5.1 %collective-permute-start.32 = (bf16[128,640]{1,0:T(8,128)(2,1)}, bf16[128,640]{1,0:T(8,128)(2,1)S(1)}, u32[]{:S(2)}, u32[]{:S(2)}) collective-permute-start(bf16[128,640]{1,0:T(8,128)(2,1)} %get-tuple-element.59), channel_id=1, source_target_pairs={{0,97},{1,98},{2,99},{3,100},{4,101},{5,102},{6,103},{7,104},{8,10... | collective-permute-start | bytes 491528 | tf_op jit(solution)/shard_map/ppermute | solution.py:29
  186.6 5.9 %collective-permute-start.34 = (bf16[128,640]{1,0:T(8,128)(2,1)}, bf16[128,640]{1,0:T(8,128)(2,1)S(1)}, u32[]{:S(2)}, u32[]{:S(2)}) collective-permute-start(bf16[128,640]{1,0:T(8,128)(2,1)} %get-tuple-element.61), channel_id=1, source_target_pairs={{0,161},{1,162},{2,163},{3,164},{4,165},{5,166},{6,167},{7,168},{8... | collective-permute-start | bytes 491528 | tf_op jit(solution)/shard_map/ppermute | solution.py:29
  192.6 12.3 %collective-permute-start.35 = (bf16[128,640]{1,0:T(8,128)(2,1)}, bf16[128,640]{1,0:T(8,128)(2,1)S(1)}, u32[]{:S(2)}, u32[]{:S(2)}) collective-permute-start(bf16[128,640]{1,0:T(8,128)(2,1)} %get-tuple-element.62), channel_id=1, source_target_pairs={{0,193},{1,194},{2,195},{3,196},{4,197},{5,198},{6,199},{7,200},{8... | collective-permute-start | bytes 491528 | tf_op jit(solution)/shard_map/ppermute | solution.py:29
  204.9 11.5 %collective-permute-done.31.refs_2_ = bf16[128,640]{1,0:T(8,128)(2,1)S(1)} collective-permute-done((bf16[128,640]{1,0:T(8,128)(2,1)}, bf16[128,640]{1,0:T(8,128)(2,1)S(1)}, u32[]{:S(2)}, u32[]{:S(2)}) %collective-permute-start.31) | collective-permute-done | bytes 163872 | tf_op jit(solution)/shard_map/ppermute | solution.py:29
  216.4 2.3 collective-permute-start.36
  218.8 2.7 %collective-permute-start.22 = (bf16[64,1024]{1,0:T(8,128)(2,1)}, bf16[64,1024]{1,0:T(8,128)(2,1)S(1)}, u32[]{:S(2)}, u32[]{:S(2)}) collective-permute-start(bf16[64,1024]{1,0:T(8,128)(2,1)} %get-tuple-element.55.refs_8_), channel_id=1, source_target_pairs={{0,64},{1,65},{2,66},{3,67},{4,68},{5,69},{6,70},{7,71},{8,72},{9,... | collective-permute-start | bytes 393224 | tf_op jit(solution)/shard_map/ppermute | solution.py:29
  221.5 4.8 %collective-permute-done.33.refs_4_ = bf16[128,640]{1,0:T(8,128)(2,1)S(1)} collective-permute-done((bf16[128,640]{1,0:T(8,128)(2,1)}, bf16[128,640]{1,0:T(8,128)(2,1)S(1)}, u32[]{:S(2)}, u32[]{:S(2)}) %collective-permute-start.33) | collective-permute-done | bytes 163872 | tf_op jit(solution)/shard_map/ppermute | solution.py:29
  228.3 2.3 collect.1
  230.6 7.3 %collective-permute-start.38 = (f32[128,128]{1,0:T(8,128)}, f32[128,128]{1,0:T(8,128)S(1)}, u32[]{:S(2)}, u32[]{:S(2)}) collective-permute-start(f32[128,128]{1,0:T(8,128)} %get-tuple-element.66), channel_id=1, source_target_pairs={{0,192},{1,193},{2,194},{3,195},{4,196},{5,197},{6,198},{7,199},{8... | collective-permute-start | bytes 196616 | tf_op jit(solution)/shard_map/ppermute | solution.py:29
  240.6 3.1 %collective-permute-start.39 = (f32[128,128]{1,0:T(8,128)}, f32[128,128]{1,0:T(8,128)S(1)}, u32[]{:S(2)}, u32[]{:S(2)}) collective-permute-start(f32[128,128]{1,0:T(8,128)} %get-tuple-element.67), channel_id=1, source_target_pairs={{0,160},{1,161},{2,162},{3,163},{4,164},{5,165},{6,166},{7,167},{8... | collective-permute-start | bytes 196616 | tf_op jit(solution)/shard_map/ppermute | solution.py:29
  250.0 10.9 %panel_rows.1 = bf16[8,128,1024]{2,1,0:T(8,128)(2,1)} custom-call(s32[3]{0:T(128)} %pad_add_fusion.where, bf16[8,128,1024]{2,1,0:T(8,128)(2,1)} %bitcast.13, bf16[1024,1024]{1,0:T(8,128)(2,1)} %bitcast.15, bf16[64,1024]{1,0:T(8,128)(2,1)} %orthonormal.1.refs_0_.basis_ref, bf16[64,1024]{1,0:T(8,128)(2,1)} %copy-done.1, bf16[64,1024]{1,0:T(8,128)(2,1)} %copy-done.2, ...), custom_call_target="tpu_custom_call" | custom-call | tf_op jit(solution)/shard_map/panel_rows/pallas_call | solution.py:268
  (139 shorter events, 34.4 us)
Async XLA Ops:
  12.6 7.0 %collective-permute-start.1 = (bf16[64,1024]{1,0:T(8,128)(2,1)}, bf16[64,1024]{1,0:T(8,128)(2,1)S(1)}, u32[]{:S(2)}, u32[]{:S(2)}) collective-permute-start(bf16[64,1024]{1,0:T(8,128)(2,1)} %get-tuple-element.38), channel_id=1, source_target_pairs={{0,64},{1,65},{2,66},{3,67},{4,68},{5,69},{6,70},{7,71},{8,72},{9,... | collective-permute-start | bytes 393224 | tf_op jit(solution)/shard_map/ppermute | solution.py:29
  14.1 9.3 %collective-permute-start.2 = (bf16[64,1024]{1,0:T(8,128)(2,1)}, bf16[64,1024]{1,0:T(8,128)(2,1)S(1)}, u32[]{:S(2)}, u32[]{:S(2)}) collective-permute-start(bf16[64,1024]{1,0:T(8,128)(2,1)} %get-tuple-element.39), channel_id=1, source_target_pairs={{0,128},{1,129},{2,130},{3,131},{4,132},{5,133},{6,134},{7,135},{8... | collective-permute-start | bytes 393224 | tf_op jit(solution)/shard_map/ppermute | solution.py:29
  34.6 8.8 %collective-permute-start.4 = (bf16[64,1024]{1,0:T(8,128)(2,1)}, bf16[64,1024]{1,0:T(8,128)(2,1)S(1)}, u32[]{:S(2)}, u32[]{:S(2)}) collective-permute-start(bf16[64,1024]{1,0:T(8,128)(2,1)} %orthonormal.1.refs_0_.basis_ref), channel_id=1, source_target_pairs={{0,64},{1,65},{2,66},{3,67},{4,68},{5,69},{6,70},{7,71},{8,72},{9,... | collective-permute-start | bytes 393224 | tf_op jit(solution)/shard_map/ppermute | solution.py:29
  34.6 8.8 %collective-permute-start.5 = (bf16[64,1024]{1,0:T(8,128)(2,1)}, bf16[64,1024]{1,0:T(8,128)(2,1)S(1)}, u32[]{:S(2)}, u32[]{:S(2)}) collective-permute-start(bf16[64,1024]{1,0:T(8,128)(2,1)} %orthonormal.1.refs_0_.basis_ref), channel_id=1, source_target_pairs={{0,128},{1,129},{2,130},{3,131},{4,132},{5,133},{6,134},{7,135},{8... | collective-permute-start | bytes 393224 | tf_op jit(solution)/shard_map/ppermute | solution.py:29
  52.7 76.5 %collective-permute-start.11 = (bf16[4,64,1024]{2,1,0:T(8,128)(2,1)}, bf16[4,64,1024]{2,1,0:T(8,128)(2,1)S(1)}, u32[]{:S(2)}, u32[]{:S(2)}) collective-permute-start(bf16[4,64,1024]{2,1,0:T(8,128)(2,1)} %get-tuple-element.42), channel_id=1, source_target_pairs={{0,32},{1,33},{2,34},{3,35},{4,36},{5,37},{6,38},{7,39},{8,40},{9,... | collective-permute-start | bytes 1572872 | tf_op jit(solution)/shard_map/ppermute | solution.py:29
  118.2 9.1 %collective-permute-start.15 = (bf16[128,1024]{1,0:T(8,128)(2,1)}, bf16[128,1024]{1,0:T(8,128)(2,1)S(1)}, u32[]{:S(2)}, u32[]{:S(2)}) collective-permute-start(bf16[128,1024]{1,0:T(8,128)(2,1)} %get-tuple-element.48), channel_id=1, source_target_pairs={{0,32},{1,33},{2,34},{3,35},{4,36},{5,37},{6,38},{7,39},{8,40},{9,... | collective-permute-start | bytes 786440 | tf_op jit(solution)/shard_map/ppermute | solution.py:29
  118.6 10.6 %collective-permute-start.16 = (bf16[128,1024]{1,0:T(8,128)(2,1)}, bf16[128,1024]{1,0:T(8,128)(2,1)S(1)}, u32[]{:S(2)}, u32[]{:S(2)}) collective-permute-start(bf16[128,1024]{1,0:T(8,128)(2,1)} %get-tuple-element.49), channel_id=1, source_target_pairs={{0,64},{1,65},{2,66},{3,67},{4,68},{5,69},{6,70},{7,71},{8,72},{9,... | collective-permute-start | bytes 786440 | tf_op jit(solution)/shard_map/ppermute | solution.py:29
  118.6 18.8 %collective-permute-start.17 = (bf16[128,1024]{1,0:T(8,128)(2,1)}, bf16[128,1024]{1,0:T(8,128)(2,1)S(1)}, u32[]{:S(2)}, u32[]{:S(2)}) collective-permute-start(bf16[128,1024]{1,0:T(8,128)(2,1)} %get-tuple-element.50), channel_id=1, source_target_pairs={{0,96},{1,97},{2,98},{3,99},{4,100},{5,101},{6,102},{7,103},{8,104... | collective-permute-start | bytes 786440 | tf_op jit(solution)/shard_map/ppermute | solution.py:29
  119.6 27.7 %collective-permute-start.18 = (bf16[128,1024]{1,0:T(8,128)(2,1)}, bf16[128,1024]{1,0:T(8,128)(2,1)S(1)}, u32[]{:S(2)}, u32[]{:S(2)}) collective-permute-start(bf16[128,1024]{1,0:T(8,128)(2,1)} %get-tuple-element.51), channel_id=1, source_target_pairs={{0,128},{1,129},{2,130},{3,131},{4,132},{5,133},{6,134},{7,135},{8... | collective-permute-start | bytes 786440 | tf_op jit(solution)/shard_map/ppermute | solution.py:29
  127.4 21.9 %collective-permute-start.19 = (bf16[128,1024]{1,0:T(8,128)(2,1)}, bf16[128,1024]{1,0:T(8,128)(2,1)S(1)}, u32[]{:S(2)}, u32[]{:S(2)}) collective-permute-start(bf16[128,1024]{1,0:T(8,128)(2,1)} %get-tuple-element.52), channel_id=1, source_target_pairs={{0,160},{1,161},{2,162},{3,163},{4,164},{5,165},{6,166},{7,167},{8... | collective-permute-start | bytes 786440 | tf_op jit(solution)/shard_map/ppermute | solution.py:29
  129.2 22.5 %collective-permute-start.20 = (bf16[128,1024]{1,0:T(8,128)(2,1)}, bf16[128,1024]{1,0:T(8,128)(2,1)S(1)}, u32[]{:S(2)}, u32[]{:S(2)}) collective-permute-start(bf16[128,1024]{1,0:T(8,128)(2,1)} %get-tuple-element.53), channel_id=1, source_target_pairs={{0,192},{1,193},{2,194},{3,195},{4,196},{5,197},{6,198},{7,199},{8... | collective-permute-start | bytes 786440 | tf_op jit(solution)/shard_map/ppermute | solution.py:29
  129.2 22.5 %collective-permute-start.21 = (bf16[128,1024]{1,0:T(8,128)(2,1)}, bf16[128,1024]{1,0:T(8,128)(2,1)S(1)}, u32[]{:S(2)}, u32[]{:S(2)}) collective-permute-start(bf16[128,1024]{1,0:T(8,128)(2,1)} %get-tuple-element.54), channel_id=1, source_target_pairs={{0,224},{1,225},{2,226},{3,227},{4,228},{5,229},{6,230},{7,231},{8... | collective-permute-start | bytes 786440 | tf_op jit(solution)/shard_map/ppermute | solution.py:29
  137.4 14.4 %collective-permute-start.12 = (bf16[64,1024]{1,0:T(8,128)(2,1)}, bf16[64,1024]{1,0:T(8,128)(2,1)S(1)}, u32[]{:S(2)}, u32[]{:S(2)}) collective-permute-start(bf16[64,1024]{1,0:T(8,128)(2,1)} %get-tuple-element.44), channel_id=1, source_target_pairs={{0,64},{1,65},{2,66},{3,67},{4,68},{5,69},{6,70},{7,71},{8,72},{9,... | collective-permute-start | bytes 393224 | tf_op jit(solution)/shard_map/ppermute | solution.py:29
  147.3 7.7 %collective-permute-start.13 = (bf16[64,1024]{1,0:T(8,128)(2,1)}, bf16[64,1024]{1,0:T(8,128)(2,1)S(1)}, u32[]{:S(2)}, u32[]{:S(2)}) collective-permute-start(bf16[64,1024]{1,0:T(8,128)(2,1)} %get-tuple-element.45), channel_id=1, source_target_pairs={{0,128},{1,129},{2,130},{3,131},{4,132},{5,133},{6,134},{7,135},{8... | collective-permute-start | bytes 393224 | tf_op jit(solution)/shard_map/ppermute | solution.py:29
  149.2 8.2 %collective-permute-start.14 = (bf16[64,1024]{1,0:T(8,128)(2,1)}, bf16[64,1024]{1,0:T(8,128)(2,1)S(1)}, u32[]{:S(2)}, u32[]{:S(2)}) collective-permute-start(bf16[64,1024]{1,0:T(8,128)(2,1)} %get-tuple-element.46), channel_id=1, source_target_pairs={{0,192},{1,193},{2,194},{3,195},{4,196},{5,197},{6,198},{7,199},{8... | collective-permute-start | bytes 393224 | tf_op jit(solution)/shard_map/ppermute | solution.py:29
  170.6 16.0 %collective-permute-start.29 = (bf16[128,640]{1,0:T(8,128)(2,1)}, bf16[128,640]{1,0:T(8,128)(2,1)S(1)}, u32[]{:S(2)}, u32[]{:S(2)}) collective-permute-start(bf16[128,640]{1,0:T(8,128)(2,1)} %get-tuple-element.56), channel_id=1, source_target_pairs={{0,1},{1,2},{2,3},{3,4},{4,5},{5,6},{6,7},{7,8},{8,9},{9,10},{10,1... | collective-permute-start | bytes 491528 | tf_op jit(solution)/shard_map/ppermute | solution.py:29
  174.1 18.5 %collective-permute-start.30 = (bf16[128,640]{1,0:T(8,128)(2,1)}, bf16[128,640]{1,0:T(8,128)(2,1)S(1)}, u32[]{:S(2)}, u32[]{:S(2)}) collective-permute-start(bf16[128,640]{1,0:T(8,128)(2,1)} %get-tuple-element.57), channel_id=1, source_target_pairs={{0,33},{1,34},{2,35},{3,36},{4,37},{5,38},{6,39},{7,40},{8,41},{9,... | collective-permute-start | bytes 491528 | tf_op jit(solution)/shard_map/ppermute | solution.py:29
  177.1 39.3 %collective-permute-start.31 = (bf16[128,640]{1,0:T(8,128)(2,1)}, bf16[128,640]{1,0:T(8,128)(2,1)S(1)}, u32[]{:S(2)}, u32[]{:S(2)}) collective-permute-start(bf16[128,640]{1,0:T(8,128)(2,1)} %get-tuple-element.58), channel_id=1, source_target_pairs={{0,65},{1,66},{2,67},{3,68},{4,69},{5,70},{6,71},{7,72},{8,73},{9,... | collective-permute-start | bytes 491528 | tf_op jit(solution)/shard_map/ppermute | solution.py:29
  179.5 39.2 %collective-permute-start.32 = (bf16[128,640]{1,0:T(8,128)(2,1)}, bf16[128,640]{1,0:T(8,128)(2,1)S(1)}, u32[]{:S(2)}, u32[]{:S(2)}) collective-permute-start(bf16[128,640]{1,0:T(8,128)(2,1)} %get-tuple-element.59), channel_id=1, source_target_pairs={{0,97},{1,98},{2,99},{3,100},{4,101},{5,102},{6,103},{7,104},{8,10... | collective-permute-start | bytes 491528 | tf_op jit(solution)/shard_map/ppermute | solution.py:29
  184.6 41.7 %collective-permute-start.33 = (bf16[128,640]{1,0:T(8,128)(2,1)}, bf16[128,640]{1,0:T(8,128)(2,1)S(1)}, u32[]{:S(2)}, u32[]{:S(2)}) collective-permute-start(bf16[128,640]{1,0:T(8,128)(2,1)} %get-tuple-element.60), channel_id=1, source_target_pairs={{0,129},{1,130},{2,131},{3,132},{4,133},{5,134},{6,135},{7,136},{8... | collective-permute-start | bytes 491528 | tf_op jit(solution)/shard_map/ppermute | solution.py:29
  186.6 39.7 %collective-permute-start.34 = (bf16[128,640]{1,0:T(8,128)(2,1)}, bf16[128,640]{1,0:T(8,128)(2,1)S(1)}, u32[]{:S(2)}, u32[]{:S(2)}) collective-permute-start(bf16[128,640]{1,0:T(8,128)(2,1)} %get-tuple-element.61), channel_id=1, source_target_pairs={{0,161},{1,162},{2,163},{3,164},{4,165},{5,166},{6,167},{7,168},{8... | collective-permute-start | bytes 491528 | tf_op jit(solution)/shard_map/ppermute | solution.py:29
  192.6 34.4 %collective-permute-start.35 = (bf16[128,640]{1,0:T(8,128)(2,1)}, bf16[128,640]{1,0:T(8,128)(2,1)S(1)}, u32[]{:S(2)}, u32[]{:S(2)}) collective-permute-start(bf16[128,640]{1,0:T(8,128)(2,1)} %get-tuple-element.62), channel_id=1, source_target_pairs={{0,193},{1,194},{2,195},{3,196},{4,197},{5,198},{6,199},{7,200},{8... | collective-permute-start | bytes 491528 | tf_op jit(solution)/shard_map/ppermute | solution.py:29
  216.4 10.6 %collective-permute-start.36 = (bf16[128,640]{1,0:T(8,128)(2,1)}, bf16[128,640]{1,0:T(8,128)(2,1)S(1)}, u32[]{:S(2)}, u32[]{:S(2)}) collective-permute-start(bf16[128,640]{1,0:T(8,128)(2,1)} %get-tuple-element.63), channel_id=1, source_target_pairs={{0,225},{1,226},{2,227},{3,228},{4,229},{5,230},{6,231},{7,232},{8... | collective-permute-start | bytes 491528 | tf_op jit(solution)/shard_map/ppermute | solution.py:29
  218.8 19.2 %collective-permute-start.22 = (bf16[64,1024]{1,0:T(8,128)(2,1)}, bf16[64,1024]{1,0:T(8,128)(2,1)S(1)}, u32[]{:S(2)}, u32[]{:S(2)}) collective-permute-start(bf16[64,1024]{1,0:T(8,128)(2,1)} %get-tuple-element.55.refs_8_), channel_id=1, source_target_pairs={{0,64},{1,65},{2,66},{3,67},{4,68},{5,69},{6,70},{7,71},{8,72},{9,... | collective-permute-start | bytes 393224 | tf_op jit(solution)/shard_map/ppermute | solution.py:29
  226.3 11.6 %collective-permute-start.23 = (bf16[64,1024]{1,0:T(8,128)(2,1)}, bf16[64,1024]{1,0:T(8,128)(2,1)S(1)}, u32[]{:S(2)}, u32[]{:S(2)}) collective-permute-start(bf16[64,1024]{1,0:T(8,128)(2,1)} %get-tuple-element.55.refs_8_), channel_id=1, source_target_pairs={{0,128},{1,129},{2,130},{3,131},{4,132},{5,133},{6,134},{7,135},{8... | collective-permute-start | bytes 393224 | tf_op jit(solution)/shard_map/ppermute | solution.py:29
  226.3 12.1 %collective-permute-start.24 = (bf16[64,1024]{1,0:T(8,128)(2,1)}, bf16[64,1024]{1,0:T(8,128)(2,1)S(1)}, u32[]{:S(2)}, u32[]{:S(2)}) collective-permute-start(bf16[64,1024]{1,0:T(8,128)(2,1)} %get-tuple-element.55.refs_8_), channel_id=1, source_target_pairs={{0,192},{1,193},{2,194},{3,195},{4,196},{5,197},{6,198},{7,199},{8... | collective-permute-start | bytes 393224 | tf_op jit(solution)/shard_map/ppermute | solution.py:29
  230.6 8.0 %collective-permute-start.37 = (f32[128,128]{1,0:T(8,128)}, f32[128,128]{1,0:T(8,128)S(1)}, u32[]{:S(2)}, u32[]{:S(2)}) collective-permute-start(f32[128,128]{1,0:T(8,128)} %get-tuple-element.65), channel_id=1, source_target_pairs={{0,224},{1,225},{2,226},{3,227},{4,228},{5,229},{6,230},{7,231},{8... | collective-permute-start | bytes 196616 | tf_op jit(solution)/shard_map/ppermute | solution.py:29
  230.6 10.0 %collective-permute-start.38 = (f32[128,128]{1,0:T(8,128)}, f32[128,128]{1,0:T(8,128)S(1)}, u32[]{:S(2)}, u32[]{:S(2)}) collective-permute-start(f32[128,128]{1,0:T(8,128)} %get-tuple-element.66), channel_id=1, source_target_pairs={{0,192},{1,193},{2,194},{3,195},{4,196},{5,197},{6,198},{7,199},{8... | collective-permute-start | bytes 196616 | tf_op jit(solution)/shard_map/ppermute | solution.py:29
  237.9 10.6 %collective-permute-start.25 = (bf16[64,1024]{1,0:T(8,128)(2,1)}, bf16[64,1024]{1,0:T(8,128)(2,1)S(1)}, u32[]{:S(2)}, u32[]{:S(2)}) collective-permute-start(bf16[64,1024]{1,0:T(8,128)(2,1)} %get-tuple-element.55.refs_8_), channel_id=1, source_target_pairs={{0,32},{1,33},{2,34},{3,35},{4,36},{5,37},{6,38},{7,39},{8,40},{9,... | collective-permute-start | bytes 393224 | tf_op jit(solution)/shard_map/ppermute | solution.py:29
  238.0 10.6 %collective-permute-start.26 = (bf16[64,1024]{1,0:T(8,128)(2,1)S(1)}, bf16[64,1024]{1,0:T(8,128)(2,1)S(1)}, u32[]{:S(2)}, u32[]{:S(2)}) collective-permute-start(bf16[64,1024]{1,0:T(8,128)(2,1)S(1)} %collective-permute-done.22.refs_9_), channel_id=1, source_target_pairs={{0,32},{1,33},{2,34},{3,35},{4,36},{5,37},{6,38},{7,39},{8,40},{9,... | collective-permute-start | bytes 393224 | tf_op jit(solution)/shard_map/ppermute | solution.py:29
  238.5 10.1 %collective-permute-start.27 = (bf16[64,1024]{1,0:T(8,128)(2,1)S(1)}, bf16[64,1024]{1,0:T(8,128)(2,1)S(1)}, u32[]{:S(2)}, u32[]{:S(2)}) collective-permute-start(bf16[64,1024]{1,0:T(8,128)(2,1)S(1)} %collective-permute-done.23.refs_10_), channel_id=1, source_target_pairs={{0,32},{1,33},{2,34},{3,35},{4,36},{5,37},{6,38},{7,39},{8,40},{9,... | collective-permute-start | bytes 393224 | tf_op jit(solution)/shard_map/ppermute | solution.py:29
  238.6 10.0 %collective-permute-start.28 = (bf16[64,1024]{1,0:T(8,128)(2,1)S(1)}, bf16[64,1024]{1,0:T(8,128)(2,1)S(1)}, u32[]{:S(2)}, u32[]{:S(2)}) collective-permute-start(bf16[64,1024]{1,0:T(8,128)(2,1)S(1)} %collective-permute-done.24.refs_11_), channel_id=1, source_target_pairs={{0,32},{1,33},{2,34},{3,35},{4,36},{5,37},{6,38},{7,39},{8,40},{9,... | collective-permute-start | bytes 393224 | tf_op jit(solution)/shard_map/ppermute | solution.py:29
  (48 other events, 320.1 us)
